TPU v7x, 32 devices: a whole 2x2x4 slice. The times are simulated.
32 devices in a mesh: grp: 2 (over core), kv: 2 (over x), srv: 8 (over z, y).
Axes of the slice: x: 2, y: 2, z: 4, core: 2. Of those that a mesh axis runs over, the one named last changes fastest.
Arguments:
- queries: bfloat16 [2048, 8, 1024], P('srv', 'kv', 'grp'), may hold values from -120 to 120
- keys: bfloat16 [2048, 8, 128], P('srv', 'kv'), may hold values from -5 to 5
- values: bfloat16 [2048, 8, 128], P('srv', 'kv'), may hold values from -6 to 6
- lengths: int32 [4], replicated, may hold values from 1 to 1024, 2048 in all
- output_projection_weight: bfloat16 [8, 1024, 8192], P('kv', 'grp', 'srv'), may hold values from -0.0625 to 0.0625
Outputs:
- projected: bfloat16 [2048, 8192], P('srv', ('grp', 'kv'))
Inputs may be any that keep to these rules, and one draw needn't show every extreme that they name: The 4 lengths sum to 2048; the longest document has exactly 1024 tokens.
All inputs are finite; a program needn't handle non-finite values.
Results may differ from a plain program's by a relative error of at most 0.017.
Values may be sent and summed in bfloat16 or wider, within the bound.
A program may use at most 128 MiB of HBM per device.

v0:
```python
import functools
import math

import jax
import jax.numpy as jnp
from jax import lax
from jax.experimental import pallas as pl
from jax.experimental.pallas import tpu as pltpu
from jax.sharding import PartitionSpec as P

REACH = 4
PIECES = 4
FAR = -1e30
MESH = pl.DeviceIdType.MESH


def layer(plan, lengths, q_ref, kv_ref, w_ref, out_ref, kvw, bias, abuf, wbuf, send1, recv1,
          acc, send2, recv2, send3, kv_s, kv_r, y_s, y_r, swap_s, swap_r, own_w, w_s, w_r,
          a_s, a_r, s1, r1, s2, r2, s3, r3):
    head, halves, lanes, pairs, chunk, own_chunks = plan
    tokens, inner = q_ref.shape
    groups = kvw.shape[3] // head
    heads = inner // (groups * head)
    span = heads * head
    chunks = wbuf.shape[0]
    columns = w_ref.shape[1]
    rows = halves * tokens
    a, g, s = lax.axis_index("grp"), lax.axis_index("kv"), lax.axis_index("srv")
    u, v = s // pairs, s % pairs
    q = a * halves + g

    core = (1 - a, g, s)
    beside = (a, g, u * pairs + 1 - v)
    ahead = (a, g, s + pairs)
    behind = (a, g, s - pairs)
    across = (u // halves, u % halves, q * pairs + v)
    away = q != u
    right, left = u + 1 < lanes, u > 0

    def other_half(k):
        return (a, (g + k) % halves, s)

    barrier = pltpu.get_barrier_semaphore()

    def greet(device):
        pl.semaphore_signal(barrier, inc=1, device_id=device, device_id_type=MESH)

    greet(core)
    greet(beside)
    for k in range(1, halves):
        greet(other_half(k))
    pl.when(right)(lambda: greet(ahead))
    pl.when(left)(lambda: greet(behind))
    pl.when(away)(lambda: greet(across))
    peers = jnp.int32(1 + halves)
    for there in (right, left, away):
        peers = peers + jnp.where(there, 1, 0)
    pl.semaphore_wait(barrier, peers)

    def remote(src, dst, send, recv, device):
        return pltpu.make_async_remote_copy(
            src_ref=src, dst_ref=dst, send_sem=send, recv_sem=recv,
            device_id=device, device_id_type=MESH,
        )

    def hop(d):
        src = kv_ref.at[a] if d == 2 else kvw.at[a, 2]
        return remote(src, kvw.at[a, d], kv_s.at[d // 2 - 1], kv_r.at[d // 2 - 1], ahead)

    def sideways(d):
        src = kv_ref.at[a] if d == 0 else kvw.at[a, d]
        slot = jnp.where(v == 0, d + 1, d - 1)
        return remote(src, kvw.at[a, slot], y_s.at[d // 2], y_r.at[slot // 2], beside)

    def came(d):
        return remote(kv_ref.at[a], kvw.at[a, d], y_s.at[0], y_r.at[d // 2], beside)

    def swap(d):
        return remote(kvw.at[a, d], kvw.at[a, d], swap_s.at[d - 1], swap_r.at[d - 1], core)

    def swapped(d):
        return remote(kvw.at[a, d], kvw.at[1 - a, d], swap_s.at[d - 1], swap_r.at[d - 1], core)

    depth = inner // PIECES

    def weight(c, p):
        part = pl.ds(p * depth, depth)
        return remote(
            w_ref.at[part, pl.ds(c * chunk, chunk)], wbuf.at[own_chunks + c, part],
            w_s.at[c, p], w_r.at[c, p], beside,
        )

    def own_weight(c):
        return pltpu.make_async_copy(
            w_ref.at[:, pl.ds(c * chunk, chunk)], wbuf.at[c], own_w.at[c]
        )

    two, four = u >= 1, u >= 2
    pl.when(right)(lambda: hop(2).start())
    pl.when(v == 0)(lambda: sideways(0).start())
    weight(0, 0).start()
    for c in range(own_chunks):
        own_weight(c).start()
    kvw[0, 0] = kv_ref[0]
    kvw[1, 0] = kv_ref[1]
    for d in range(1, REACH + 1):
        @pl.when(s < d)
        def _():
            kvw[0, d] = jnp.zeros(kvw.shape[2:], kvw.dtype)
            kvw[1, d] = jnp.zeros(kvw.shape[2:], kvw.dtype)

    row = lax.broadcasted_iota(jnp.int32, (tokens, 1), 0)
    query_pos = s * tokens + row
    first = jnp.zeros((tokens, 1), jnp.int32)
    start = jnp.int32(0)
    for i in range(lengths.shape[0]):
        first = jnp.where(query_pos >= start, start, first)
        start = start + lengths[i]
    lane = lax.broadcasted_iota(jnp.int32, (tokens, tokens), 1)
    for d in range(REACH + 1):
        key_pos = (s - d) * tokens + lane
        allowed = (key_pos >= first) & (key_pos <= query_pos)
        bias[:, d * tokens:(d + 1) * tokens] = jnp.where(allowed, 0.0, FAR)

    @pl.when(two)
    def _():
        hop(2).wait_recv()
        pl.when(right)(lambda: hop(4).start())
        sideways(2).start()
        swap(2).start()

    weight(0, 1).start()

    @pl.when(s >= 1)
    def _():
        came(1).wait_recv()
        swap(1).start()

    @pl.when(four)
    def _():
        hop(4).wait_recv()
        pl.when(v == 1)(lambda: sideways(4).start())
        swap(4).start()

    for p in range(2, PIECES):
        weight(0, p).start()
    for c in range(1, own_chunks):
        for p in range(PIECES):
            weight(c, p).start()

    @pl.when(s >= 3)
    def _():
        came(3).wait_recv()
        swap(3).start()

    for d in range(1, REACH + 1):
        pl.when(s >= d)(lambda d=d: swapped(d).wait_recv())

    def relay(way, d, j):
        block = u - (d - 1) if way == 0 else u + (d - 1)
        part = abuf.at[block, :, pl.ds(pl.multiple_of(j * span, span), span)]
        return remote(part, part, a_s.at[way, d - 1, j], a_r.at[way, d - 1, j],
                      ahead if way == 0 else behind)

    def relayed(way, d, j):
        block = u - d if way == 0 else u + d
        part = abuf.at[block, :, pl.ds(pl.multiple_of(j * span, span), span)]
        return remote(part, part, a_s.at[way, d - 1, j], a_r.at[way, d - 1, j],
                      behind if way == 0 else ahead)

    def holds(way, d):
        return u >= d if way == 0 else u + d < lanes

    def may_send(way):
        return right if way == 0 else left

    def forward(d, j):
        for way in range(2):
            @pl.when(holds(way, d - 1))
            def _():
                relayed(way, d - 1, j).wait_recv()
                pl.when(may_send(way))(lambda: relay(way, d, j).start())

    factor = math.log2(math.e) / math.sqrt(head)

    def per_group(j, carry):
        at = pl.ds(pl.multiple_of(j * head, head), head)

        def per_head(h, inside):
            mine = pl.ds(pl.multiple_of(j * span + h * head, head), head)
            window = kvw[0, :, :, at].reshape((REACH + 1) * tokens, head)
            scores = lax.dot_general(
                q_ref[:, mine], window, (((1,), (1,)), ((), ())),
                preferred_element_type=jnp.float32,
            ) + bias[...]
            peak = jnp.max(scores, axis=1, keepdims=True)
            weights = jnp.exp2((scores - peak) * factor)
            total = jnp.sum(weights, axis=1, keepdims=True)
            numer = jnp.dot(
                weights.astype(jnp.bfloat16),
                kvw[1, :, :, at].reshape((REACH + 1) * tokens, head),
                preferred_element_type=jnp.float32,
            )
            abuf[u, :, mine] = (numer / total).astype(abuf.dtype)
            return inside

        lax.fori_loop(0, heads, per_head, 0)
        for way in range(2):
            pl.when(may_send(way))(lambda: relay(way, 1, j).start())
        pl.when(j >= 2)(lambda: forward(2, j - 2))
        return carry

    lax.fori_loop(0, groups, per_group, 0)

    def over_groups(low, body):
        def step(j, carry):
            body(j)
            return carry

        lax.fori_loop(low, groups, step, 0)

    over_groups(max(0, groups - 2), lambda j: forward(2, j))
    for d in range(3, lanes):
        over_groups(0, lambda j: forward(d, j))

    def last(j):
        for way in range(2):
            pl.when(holds(way, lanes - 1))(lambda: relayed(way, lanes - 1, j).wait_recv())

    over_groups(0, last)

    def to_core(c):
        return remote(send1.at[c], recv1.at[c], s1.at[c], r1.at[c], core)

    def to_half(c, k):
        return remote(send2.at[c, pl.ds((g + k) % halves * tokens, tokens)], recv2.at[c, k - 1],
                      s2.at[c, k - 1], r2.at[c, k - 1], other_half(k))

    def result(c):
        own = c < own_chunks
        offset = jnp.where(own, v * columns + c * chunk,
                           (1 - v) * columns + (c - own_chunks) * chunk)
        return out_ref.at[:, pl.ds(pl.multiple_of(offset, chunk), chunk)]

    def to_owner(c):
        return remote(send3.at[c], result(c), s3.at[c], r3.at[c], across)

    def to_self(c):
        return pltpu.make_async_copy(send3.at[c], result(c), r3.at[c])

    def product(half, c):
        left_side = abuf[pl.ds(half * halves, halves)].reshape(rows, inner)
        return jnp.dot(left_side, wbuf[c], preferred_element_type=jnp.float32)

    def second(c):
        for k in range(1, halves):
            to_half(c, k).wait_recv()
        total = acc[c, pl.ds(g * tokens, tokens)]
        for k in range(1, halves):
            total = total + recv2[c, k - 1].astype(jnp.float32)
        send3[c] = total.astype(send3.dtype)
        pl.when(away)(lambda: to_owner(c).start())
        pl.when(jnp.logical_not(away))(lambda: to_self(c).start())

    def per_chunk(c, carry):
        pl.when(c < own_chunks)(lambda: own_weight(c).wait())

        @pl.when(c >= own_chunks)
        def _():
            for p in range(PIECES):
                weight(c - own_chunks, p).wait_recv()

        send1[c] = product(1 - a, c).astype(send1.dtype)
        to_core(c).start()
        acc[c] = product(a, c)
        pl.when(c >= 1)(lambda: second(c - 1))
        to_core(c).wait_recv()
        total = acc[c] + recv1[c].astype(jnp.float32)
        acc[c] = total
        send2[c] = total.astype(send2.dtype)
        for k in range(1, halves):
            to_half(c, k).start()
        return carry

    lax.fori_loop(0, chunks, per_chunk, 0)
    second(chunks - 1)

    pl.when(right)(lambda: hop(2).wait_send())
    pl.when(two & right)(lambda: hop(4).wait_send())
    pl.when(v == 0)(lambda: sideways(0).wait_send())
    pl.when(two)(lambda: sideways(2).wait_send())
    pl.when(four & (v == 1))(lambda: sideways(4).wait_send())
    for d in range(1, REACH + 1):
        pl.when(s >= d)(lambda d=d: swap(d).wait_send())
    for c in range(own_chunks):
        for p in range(PIECES):
            weight(c, p).wait_send()
    for d in range(1, lanes):
        for way in range(2):
            @pl.when(holds(way, d - 1) & may_send(way))
            def _():
                over_groups(0, lambda j: relay(way, d, j).wait_send())

    def finish(c, carry):
        to_core(c).wait_send()
        for k in range(1, halves):
            to_half(c, k).wait_send()

        @pl.when(away)
        def _():
            to_owner(c).wait_send()
            to_owner(c).wait_recv()

        pl.when(jnp.logical_not(away))(lambda: to_self(c).wait())
        return carry

    lax.fori_loop(0, chunks, finish, 0)


def on_device(queries, keys, values, lengths, output_projection_weight):
    tokens = queries.shape[0]
    cores, halves = lax.axis_size("grp"), lax.axis_size("kv")
    lanes = cores * halves
    pairs = lax.axis_size("srv") // lanes
    assert cores == 2 and pairs == 2
    q = queries.reshape(tokens, -1)
    inner = q.shape[1]
    kv = jnp.stack([keys.reshape(tokens, -1), values.reshape(tokens, -1)])
    weight = output_projection_weight.reshape(inner, -1)
    columns = weight.shape[1]
    chunk = max(128, columns // 4)
    own_chunks = columns // chunk
    chunks = own_chunks * pairs
    groups, head = keys.shape[1], keys.shape[2]
    rows = halves * tokens
    dma = pltpu.SemaphoreType.DMA
    bf16, f32 = jnp.bfloat16, jnp.float32
    vmem = pl.BlockSpec(memory_space=pltpu.VMEM)
    return pl.pallas_call(
        functools.partial(layer, (head, halves, lanes, pairs, chunk, own_chunks)),
        out_shape=jax.ShapeDtypeStruct((tokens, pairs * columns), bf16),
        in_specs=[
            pl.BlockSpec(memory_space=pltpu.SMEM), vmem, vmem,
            pl.BlockSpec(memory_space=pl.ANY),
        ],
        out_specs=pl.BlockSpec(memory_space=pl.ANY),
        scratch_shapes=[
            pltpu.VMEM((2, REACH + 1, tokens, kv.shape[2]), bf16),
            pltpu.VMEM((tokens, (REACH + 1) * tokens), f32),
            pltpu.VMEM((lanes, tokens, inner), bf16),
            pltpu.VMEM((chunks, inner, chunk), bf16),
            pltpu.VMEM((chunks, rows, chunk), bf16),
            pltpu.VMEM((chunks, rows, chunk), bf16),
            pltpu.VMEM((chunks, rows, chunk), f32),
            pltpu.VMEM((chunks, rows, chunk), bf16),
            pltpu.VMEM((chunks, halves - 1, tokens, chunk), bf16),
            pltpu.VMEM((chunks, tokens, chunk), bf16),
            dma((2,)), dma((2,)), dma((3,)), dma((2,)), dma((REACH,)), dma((REACH,)),
            dma((own_chunks,)), dma((own_chunks, PIECES)), dma((own_chunks, PIECES)),
            dma((2, lanes - 1, groups)), dma((2, lanes - 1, groups)),
            dma((chunks,)), dma((chunks,)),
            dma((chunks, halves - 1)), dma((chunks, halves - 1)),
            dma((chunks,)), dma((chunks,)),
        ],
        compiler_params=pltpu.CompilerParams(
            collective_id=0, has_side_effects=True, vmem_limit_bytes=60 * 1024 * 1024
        ),
    )(lengths, q, kv, weight)


def solution(mesh):
    placed = (
        P("srv", "kv", "grp"),
        P("srv", "kv", None),
        P("srv", "kv", None),
        P(),
        P("kv", "grp", "srv"),
    )
    return jax.shard_map(
        on_device, mesh=mesh, in_specs=placed, out_specs=P("srv", ("grp", "kv")), check_vma=False
    )
```

profile of v0, /device:TPU:3, one launch (start us, length us, event | category | flops | bytes accessed | tf_op | source)
XLA Modules:
  0.0 177.1 jit_solution(10129911300932515679)
XLA Ops:
  0.0 1.1 stack_reshape.6
  1.1 1.1 stack_reshape.7
  2.1 0.9 pad_maximum_fusion.kv_ref
  3.0 2.5 %copy.6 = bf16[32,8,4,512]{3,1,2,0:T(8,128)(2,1)} copy(bf16[32,8,4,512]{3,2,1,0:T(4,128)(2,1)} %bitcast.5) | data formatting | bytes 2097152
  5.4 169.3 %shard_map.55 = bf16[256,2048]{1,0:T(8,128)(2,1)} custom-call(s32[4]{0:T(128)} %lengths.1, bf16[256,2048]{1,0:T(8,128)(2,1)} %bitcast.4, bf16[2,256,512]{2,1,0:T(8,128)(2,1)} %pad_maximum_fusion.kv_ref, bf16[2048,1024]{1,0:T(8,128)(2,1)} %bitcast.3), custom_call_target="tpu_custom_call" | custom-call | tf_op jit(solution)/shard_map/pallas_call | solution.py:339
  174.8 2.3 %copy.8 = bf16[256,2048]{1,0:T(8,128)(2,1)} copy(bf16[256,2048]{1,0:T(8,128)(2,1)} %shard_map.55) | data formatting | bytes 2097152
where the time goes:
time: 177 us
  Pallas kernels  169 us (95%)
  local copies, waits for them, and re-layouts  6.88 us (4%)
    pallas_call x1, Pallas kernels, on_device(): pl.pallas_call(functools.partial(layer, (head, halves, lanes, pairs, chun...  169 us
    unnamed x2, local copies, waits for them, and re-layouts  4.78 us

commit v1 on v0

v1 whole, which is shorter than its diff:
```python
import functools
import math

import jax
import jax.numpy as jnp
from jax import lax
from jax.experimental import pallas as pl
from jax.experimental.pallas import tpu as pltpu
from jax.sharding import PartitionSpec as P

REACH = 4
EARLY = 2
FAR = -1e30
MESH = pl.DeviceIdType.MESH


def layer(plan, lengths, q_ref, kv_ref, w_ref, out_ref, kvw, qbuf, bias, abuf, wbuf, acc,
          send1, recv1, send2, recv2, send3, recv3, send4,
          ky_s, ky_r, kz_s, kz_r, sw_s, sw_r, q_s, q_r, own_w, w_s, w_r, a_s, a_r,
          s1, r1, s2, r2, s3, r3, s4, r4):
    head, heads, kvh, hp, hpp, halves, lanes, pairs, cw = plan
    tokens = q_ref.shape[0]
    inner = hp * head
    width = kvh * head
    split_kv = kv_ref.shape[2] > width
    own_chunks = w_ref.shape[1] // cw
    chunks = own_chunks * pairs
    items = lanes * pairs * chunks
    early = EARLY * pairs * own_chunks
    back = REACH // pairs
    half_pieces = hp // hpp
    pieces = half_pieces * pairs
    piece = hpp * head
    lag = min(4, pieces)
    per_kv = hp // kvh
    part = tokens // lanes
    a, g, s = lax.axis_index("grp"), lax.axis_index("kv"), lax.axis_index("srv")
    u, v = s // pairs, s % pairs
    q = a * halves + g
    ov = 1 - v

    core = (1 - a, g, s)
    beside = (a, g, u * pairs + ov)
    ahead = (a, g, s + pairs)
    behind = (a, g, s - pairs)
    right, left = u + 1 < lanes, u > 0
    at_home = q == u

    def other_half(k):
        return (a, (g + k) % halves, s)

    def owner(p):
        return (u // halves, u % halves, p * pairs + v)

    def giver(p):
        return (p // halves, p % halves, q * pairs + v)

    barrier = pltpu.get_barrier_semaphore()

    def greet(device):
        pl.semaphore_signal(barrier, inc=1, device_id=device, device_id_type=MESH)

    greet(core)
    greet(beside)
    for k in range(1, halves):
        greet(other_half(k))
    pl.when(right)(lambda: greet(ahead))
    pl.when(left)(lambda: greet(behind))
    for p in range(lanes):
        pl.when(jnp.logical_not(at_home & (q == p)))(lambda p=p: greet(giver(p)))
    peers = jnp.int32(1 + halves + lanes)
    peers = peers + jnp.where(right, 1, 0) + jnp.where(left, 1, 0) - jnp.where(at_home, 1, 0)

    def remote(src, dst, send, recv, device):
        return pltpu.make_async_remote_copy(
            src_ref=src, dst_ref=dst, send_sem=send, recv_sem=recv,
            device_id=device, device_id_type=MESH,
        )

    def lane_at(i, size):
        return pl.ds(pl.multiple_of(i, head), size)

    def kv_from(half, j):
        offset = half * width + j * head if split_kv else j * head
        return kv_ref.at[a, :, lane_at(offset, head)]

    def kv_at(m, back_by, w, j):
        return kvw.at[m, (back - back_by) * pairs + w, :, pl.ds(j * head, head)]

    def whose(w):
        return v if w == 0 else ov

    def kv_beside(j):
        return remote(kv_from(ov, j), kv_at(a, 0, v, j), ky_s.at[j], ky_r.at[j], beside)

    def kv_came(j):
        return remote(kv_from(ov, j), kv_at(a, 0, ov, j), ky_s.at[j], ky_r.at[j], beside)

    def kv_up(d, w, j):
        src = kv_from(v, j) if d == 1 and w == 0 else kv_at(a, d - 1, whose(w), j)
        return remote(src, kv_at(a, d, whose(w), j), kz_s.at[d - 1, w, j], kz_r.at[d - 1, w, j],
                      ahead)

    def swap(d, w, j, m):
        i = 0 if d == 0 else 2 * d - 1 + w
        ref = kv_at(m, d, whose(w), j)
        return remote(ref, ref, sw_s.at[i, j], sw_r.at[i, j], core)

    def query(j):
        size = per_kv * head
        return remote(q_ref.at[:, lane_at(ov * inner + j * size, size)],
                      qbuf.at[0, :, pl.ds(j * size, size)], q_s.at[j], q_r.at[j], beside)

    def weight(c):
        return remote(w_ref.at[pl.ds(ov * inner, inner), pl.ds(c * cw, cw)],
                      wbuf.at[own_chunks + c], w_s.at[c], w_r.at[c], beside)

    def own_weight(c):
        return pltpu.make_async_copy(
            w_ref.at[pl.ds(v * inner, inner), pl.ds(c * cw, cw)], wbuf.at[c], own_w.at[c])

    for c in range(own_chunks):
        own_weight(c).start()

    pl.semaphore_wait(barrier, peers)

    for j in range(kvh):
        kv_beside(j).start()
        pl.when(right)(lambda j=j: kv_up(1, 0, j).start())
        query(j).start()
    for c in range(own_chunks):
        weight(c).start()

    for m in range(2):
        offset = v * width if split_kv else 0
        kvw[m, back * pairs + v] = kv_ref[m, :, lane_at(offset, width)]
    qbuf[1] = q_ref[:, lane_at(v * inner, inner)]
    for d in range(1, back + 1):
        @pl.when(u < d)
        def _():
            for m in range(2):
                for w in range(pairs):
                    kvw[m, (back - d) * pairs + w] = jnp.zeros((tokens, width), kvw.dtype)

    row = lax.broadcasted_iota(jnp.int32, (tokens, 1), 0)
    lane = lax.broadcasted_iota(jnp.int32, (tokens, tokens), 1)
    for h in range(pairs):
        shard = u * pairs + (ov if h == 0 else v)
        query_pos = shard * tokens + row
        first = jnp.zeros((tokens, 1), jnp.int32)
        start = jnp.int32(0)
        for i in range(lengths.shape[0]):
            first = jnp.where(query_pos >= start, start, first)
            start = start + lengths[i]
        for d in range(REACH + 1):
            key_pos = (shard - REACH + d) * tokens + lane
            allowed = (key_pos >= first) & (key_pos <= query_pos)
            bias[h, :, d * tokens:(d + 1) * tokens] = jnp.where(allowed, 0.0, FAR)

    def kv_phase(j):
        kv_came(j).wait_recv()
        pl.when(right)(lambda: kv_up(1, 1, j).start())
        swap(0, 1, j, a).start()
        for d in range(1, back + 1):
            @pl.when(u >= d)
            def _():
                for w in range(pairs):
                    kv_up(d, w, j).wait_recv()
                    if d < back:
                        pl.when(right)(lambda w=w: kv_up(d + 1, w, j).start())
                    swap(d, w, j, a).start()

    def kv_ready(j):
        swap(0, 1, j, 1 - a).wait_recv()
        for d in range(1, back + 1):
            @pl.when(u >= d)
            def _():
                for w in range(pairs):
                    swap(d, w, j, 1 - a).wait_recv()

    def bit(p, i):
        h, r = i // half_pieces, i % half_pieces
        return abuf.at[p, jnp.where(h == 0, ov, v), :, lane_at(r * piece, piece)]

    def relay(way, d, i):
        p = u - (d - 1) if way == 0 else u + (d - 1)
        return remote(bit(p, i), bit(p, i), a_s.at[way, d - 1, i], a_r.at[way, d - 1, i],
                      ahead if way == 0 else behind)

    def relayed(way, d, i):
        p = u - d if way == 0 else u + d
        return remote(bit(p, i), bit(p, i), a_s.at[way, d - 1, i], a_r.at[way, d - 1, i],
                      behind if way == 0 else ahead)

    def holds(way, d):
        return u >= d if way == 0 else u + d < lanes

    def may_send(way):
        return right if way == 0 else left

    def forward(d, i):
        for way in range(2):
            @pl.when(holds(way, d - 1) & may_send(way))
            def _():
                relayed(way, d - 1, i).wait_recv()
                relay(way, d, i).start()

    factor = math.log2(math.e) / math.sqrt(head)
    kv_phase(0)
    kv_ready(0)

    def per_unit(i, carry):
        h, hh = i // hp, i % hp
        vv = jnp.where(h == 0, ov, v)
        for j in range(kvh):
            if j > 0:
                pl.when(i == (j - 1) * per_kv + min(2, per_kv - 1))(lambda: kv_phase(j))
                pl.when(i == j * per_kv)(lambda: kv_ready(j))
            pl.when(i == j * per_kv)(lambda: query(j).wait_recv())
        mine = lane_at(hh * head, head)
        at = lane_at((hh // heads) * head, head)
        window = kvw[0, pl.ds(vv, REACH + 1), :, at].reshape((REACH + 1) * tokens, head)
        scores = lax.dot_general(
            qbuf[h, :, mine], window, (((1,), (1,)), ((), ())),
            preferred_element_type=jnp.float32,
        ) + bias[h]
        peak = jnp.max(scores, axis=1, keepdims=True)
        weights = jnp.exp2((scores - peak) * factor)
        total = jnp.sum(weights, axis=1, keepdims=True)
        numer = jnp.dot(
            weights.astype(jnp.bfloat16),
            kvw[1, pl.ds(vv, REACH + 1), :, at].reshape((REACH + 1) * tokens, head),
            preferred_element_type=jnp.float32,
        )
        abuf[u, vv, :, mine] = (numer / total).astype(abuf.dtype)

        @pl.when(i % hpp == hpp - 1)
        def _():
            n = i // hpp
            for way in range(2):
                pl.when(may_send(way))(lambda: relay(way, 1, n).start())
            pl.when(n >= lag)(lambda: forward(2, n - lag))

        return carry

    lax.fori_loop(0, hp * pairs, per_unit, 0)

    def plane(k):
        low = jnp.minimum(u, lanes - 1 - u)
        zigzag = jnp.where(k % 2 == 1, u - (k + 1) // 2, u + k // 2)
        line = jnp.where(u < lanes - 1 - u, k, lanes - 1 - k)
        return jnp.where(k <= 2 * low, zigzag, line)

    def decode(n):
        m = n - early
        r = n - EARLY * pairs * chunks
        late = n >= EARLY * pairs * chunks
        first = n < early
        k = jnp.where(first, n // (pairs * own_chunks),
                      jnp.where(late, EARLY + r // (pairs * chunks), m % (pairs * EARLY) // pairs))
        h = jnp.where(first, n // own_chunks % pairs,
                      jnp.where(late, r // chunks % pairs, m % pairs))
        c = jnp.where(first, n % own_chunks,
                      jnp.where(late, r % chunks, own_chunks + m // (pairs * EARLY)))
        return k, h, c

    def column(c):
        return jnp.where(c < own_chunks, v * own_chunks + c, ov * own_chunks + c - own_chunks)

    def to_core(n):
        return remote(send1.at[n], recv1.at[n], s1.at[n], r1.at[n], core)

    def to_half(n, k):
        rows = pl.ds((g + k) % halves * part, part)
        return remote(send2.at[n, rows], recv2.at[n, k - 1], s2.at[n], r2.at[n], other_half(k))

    def all_halves(n):
        return remote(recv2.at[n], recv2.at[n], s2.at[n], r2.at[n], other_half(1))

    def to_beside(k, c):
        return remote(send3.at[k, c], recv3.at[k, c], s3.at[k, c], r3.at[k, c], beside)

    def result(giver_index, c):
        return out_ref.at[pl.ds(giver_index * part, part), lane_at(c * cw, cw)]

    def to_owner(k, c):
        return remote(send4.at[k, c], result(q, c), s4.at[k, c], r4.at[q, c], owner(plane(k)))

    def to_self(c):
        return pltpu.make_async_copy(send4.at[0, c], result(q, c), r4.at[q, c])

    def given(p, c):
        return remote(send4.at[0, c], result(p, c), s4.at[0, c], r4.at[p, c], giver(p))

    def stage1(n):
        k, h, c = decode(n)
        product = jnp.dot(abuf[plane(k), jnp.where(h == 0, ov, v)], wbuf[c],
                          preferred_element_type=jnp.float32)
        low, high = product[:tokens // 2], product[tokens // 2:]
        acc[n] = jnp.where(a == 0, low, high)
        send1[n] = jnp.where(a == 0, high, low).astype(send1.dtype)
        to_core(n).start()

    def stage2(n):
        to_core(n).wait_recv()
        total = acc[n] + recv1[n].astype(jnp.float32)
        acc[n] = total
        send2[n] = total.astype(send2.dtype)
        for k in range(1, halves):
            to_half(n, k).start()

    kept = pl.ds(g * part, part)

    def stage3(n):
        k, h, c = decode(n)
        if halves > 1:
            all_halves(n).wait_recv()
        total = acc[n, kept]
        for i in range(halves - 1):
            total = total + recv2[n, i].astype(jnp.float32)

        @pl.when(h == 0)
        def _():
            send3[k, column(c)] = total.astype(send3.dtype)
            to_beside(k, column(c)).start()

        @pl.when(h != 0)
        def _():
            acc[n, kept] = total

    def stage4(n, k, c):
        col = column(c)
        to_beside(k, col).wait_recv()
        total = acc[n, kept] + recv3[k, col].astype(jnp.float32)
        send4[k, col] = total.astype(send4.dtype)
        pl.when(at_home & (k == 0))(lambda: to_self(col).start())
        pl.when(jnp.logical_not(at_home & (k == 0)))(lambda: to_owner(k, col).start())

    def arrived(k, h):
        p = plane(k)
        up = p < u
        d = jnp.where(up, u - p, p - u)
        way = jnp.where(up, 0, 1)

        @pl.when(jnp.logical_not(jnp.where(up, right, left)))
        def _():
            def one(r, carry):
                i = h * half_pieces + r
                remote(bit(p, i), bit(p, i), a_s.at[way, d - 1, i], a_r.at[way, d - 1, i],
                       core).wait_recv()
                return carry

            lax.fori_loop(0, half_pieces, one, 0)

    first_end = EARLY * chunks

    def per_item(n, carry):
        k, h, c = decode(n)
        pl.when(n < lag)(lambda: forward(2, pieces - lag + n))
        if lanes > 3:
            pl.when((n >= lag) & (n < lag + pieces))(lambda: forward(3, n - lag))
        if lanes > 4:
            @pl.when(n == lag + pieces)
            def _():
                for d in range(4, lanes):
                    def one(i, carry):
                        forward(d, i)
                        return carry

                    lax.fori_loop(0, pieces, one, 0)

        for i in range(own_chunks):
            pl.when(n == i)(lambda i=i: own_weight(i).wait())
            pl.when(n == early + i * pairs * EARLY)(lambda i=i: weight(i).wait_recv())
        fresh = (n < items) & (c == 0) & (k > 0) & (h < pairs)

        @pl.when(fresh)
        def _():
            stage2(n - 1)
            arrived(k, h)

        pl.when(n < items)(lambda: stage1(n))
        pl.when(jnp.logical_not(fresh) & (n >= 1) & (n <= items))(lambda: stage2(n - 1))
        pl.when((n >= 3) & (n < items + 3))(lambda: stage3(n - 3))
        m = n - (first_end + EARLY * own_chunks + 2)

        @pl.when((m >= 0) & (m < first_end))
        def _():
            mk, mc = m // chunks, m % chunks
            index = jnp.where(mc < own_chunks, mk * pairs * own_chunks + own_chunks + mc,
                              early + (mc - own_chunks) * pairs * EARLY + mk * pairs + 1)
            stage4(index, mk, mc)

        lk, lh, lc = decode(n - 4)
        pl.when((n - 4 >= EARLY * pairs * chunks) & (lh == 1))(lambda: stage4(n - 4, lk, lc))
        return carry

    lax.fori_loop(0, items + 4, per_item, 0)

    for j in range(kvh):
        kv_beside(j).wait_send()
        query(j).wait_send()
        swap(0, 1, j, a).wait_send()
        for d in range(1, back + 1):
            for w in range(pairs):
                pl.when((u >= d - 1) & right)(lambda d=d, w=w, j=j: kv_up(d, w, j).wait_send())
                pl.when(u >= d)(lambda d=d, w=w, j=j: swap(d, w, j, a).wait_send())
    for c in range(own_chunks):
        weight(c).wait_send()
    for d in range(1, lanes):
        for way in range(2):
            @pl.when(holds(way, d - 1) & may_send(way))
            def _():
                def one(i, carry):
                    relay(way, d, i).wait_send()
                    return carry

                lax.fori_loop(0, pieces, one, 0)

    def sent(n, carry):
        to_core(n).wait_send()
        if halves > 1:
            all_halves(n).wait_send()
        return carry

    lax.fori_loop(0, items, sent, 0)

    def finish(i, carry):
        k, c = i // chunks, i % chunks
        to_beside(k, c).wait_send()
        pl.when(jnp.logical_not(at_home & (k == 0)))(lambda: to_owner(k, c).wait_send())
        pl.when(at_home & (k == q))(lambda: to_self(c).wait())
        pl.when(jnp.logical_not(at_home & (k == q)))(lambda: given(k, c).wait_recv())
        return carry

    lax.fori_loop(0, lanes * chunks, finish, 0)


def on_device(queries, keys, values, lengths, output_projection_weight):
    tokens = queries.shape[0]
    cores, halves = lax.axis_size("grp"), lax.axis_size("kv")
    lanes = cores * halves
    pairs = lax.axis_size("srv") // lanes
    assert cores == 2 and pairs == 2 and lanes > 2
    q = queries.reshape(tokens, -1)
    kv = jnp.stack([keys.reshape(tokens, -1), values.reshape(tokens, -1)])
    groups, head = keys.shape[1], keys.shape[2]
    inner = q.shape[1]
    weight = output_projection_weight.reshape(inner, -1)
    columns = weight.shape[1]
    heads = inner // (groups * head)
    kvh = max(1, groups // pairs)
    hp = inner // head // pairs
    hpp = 2
    cw = max(256, columns // 2)
    own_chunks = columns // cw
    chunks = own_chunks * pairs
    items = lanes * pairs * chunks
    pieces = hp // hpp * pairs
    part = tokens // lanes
    back = REACH // pairs
    width = kvh * head
    dma = pltpu.SemaphoreType.DMA
    bf16, f32 = jnp.bfloat16, jnp.float32
    vmem = pl.BlockSpec(memory_space=pltpu.VMEM)
    return pl.pallas_call(
        functools.partial(layer, (head, heads, kvh, hp, hpp, halves, lanes, pairs, cw)),
        out_shape=jax.ShapeDtypeStruct((tokens, pairs * columns), bf16),
        in_specs=[
            pl.BlockSpec(memory_space=pltpu.SMEM), vmem, vmem,
            pl.BlockSpec(memory_space=pl.ANY),
        ],
        out_specs=pl.BlockSpec(memory_space=pl.ANY),
        scratch_shapes=[
            pltpu.VMEM((2, (back + 1) * pairs, tokens, width), bf16),
            pltpu.VMEM((pairs, tokens, hp * head), bf16),
            pltpu.VMEM((pairs, tokens, (REACH + 1) * tokens), f32),
            pltpu.VMEM((lanes, pairs, tokens, hp * head), bf16),
            pltpu.VMEM((chunks, hp * head, cw), bf16),
            pltpu.VMEM((items, tokens // cores, cw), f32),
            pltpu.VMEM((items, tokens // cores, cw), bf16),
            pltpu.VMEM((items, tokens // cores, cw), bf16),
            pltpu.VMEM((items, tokens // cores, cw), bf16),
            pltpu.VMEM((items, halves - 1, part, cw), bf16),
            pltpu.VMEM((lanes, chunks, part, cw), bf16),
            pltpu.VMEM((lanes, chunks, part, cw), bf16),
            pltpu.VMEM((lanes, chunks, part, cw), bf16),
            dma((kvh,)), dma((kvh,)), dma((back, pairs, kvh)), dma((back, pairs, kvh)),
            dma((2 * back + 1, kvh)), dma((2 * back + 1, kvh)), dma((kvh,)), dma((kvh,)),
            dma((own_chunks,)), dma((own_chunks,)), dma((own_chunks,)),
            dma((2, lanes - 1, pieces)), dma((2, lanes - 1, pieces)),
            dma((items,)), dma((items,)), dma((items,)), dma((items,)),
            dma((lanes, chunks)), dma((lanes, chunks)), dma((lanes, chunks)), dma((lanes, chunks)),
        ],
        compiler_params=pltpu.CompilerParams(
            collective_id=0, has_side_effects=True, vmem_limit_bytes=60 * 1024 * 1024
        ),
    )(lengths, q, kv, weight)


def solution(mesh):
    placed = (
        P("srv", "kv", "grp"),
        P("srv", "kv", None),
        P("srv", "kv", None),
        P(),
        P("kv", "grp", "srv"),
    )
    return jax.shard_map(
        on_device, mesh=mesh, in_specs=placed, out_specs=P("srv", ("grp", "kv")), check_vma=False
    )
```

time: 177 us -> 138 us (0.78)
  the two profiles are of different devices: /device:TPU:3 before, /device:TPU:5 now
where the time goes in v1:
time: 138 us
  Pallas kernels  130 us (94%)
  local copies, waits for them, and re-layouts  6.88 us (5%)
    pallas_call x1, Pallas kernels, on_device(): pl.pallas_call(functools.partial(layer, (head, heads, kvh, hp, hpp, halve...  130 us
    unnamed x2, local copies, waits for them, and re-layouts  4.78 us

profile of v1, /device:TPU:5, one launch (start us, length us, event | category | flops | bytes accessed | tf_op | source)
XLA Modules:
  0.0 137.6 jit_solution(2858225292688448376)
XLA Ops:
  0.0 1.1 stack_reshape.6
  1.1 1.1 stack_reshape.7
  2.1 0.9 pad_maximum_fusion.kv_ref
  3.0 2.5 %copy.6 = bf16[32,8,4,512]{3,1,2,0:T(8,128)(2,1)} copy(bf16[32,8,4,512]{3,2,1,0:T(4,128)(2,1)} %bitcast.5) | data formatting | bytes 2097152
  5.4 129.8 %shard_map.55 = bf16[256,2048]{1,0:T(8,128)(2,1)} custom-call(s32[4]{0:T(128)} %lengths.1, bf16[256,2048]{1,0:T(8,128)(2,1)} %bitcast.4, bf16[2,256,512]{2,1,0:T(8,128)(2,1)} %pad_maximum_fusion.kv_ref, bf16[2048,1024]{1,0:T(8,128)(2,1)} %bitcast.3), custom_call_target="tpu_custom_call" | custom-call | tf_op jit(solution)/shard_map/pallas_call | solution.py:466
  135.3 2.3 %copy.8 = bf16[256,2048]{1,0:T(8,128)(2,1)} copy(bf16[256,2048]{1,0:T(8,128)(2,1)} %shard_map.55) | data formatting | bytes 2097152

commit v2 on v1

--- a/solution.py
+++ b/solution.py
@@ -9,13 +9,14 @@
 from jax.sharding import PartitionSpec as P
 
 REACH = 4
-EARLY = 2
+EARLY = 3
 FAR = -1e30
+LAG = 5
 MESH = pl.DeviceIdType.MESH
 
 
 def layer(plan, lengths, q_ref, kv_ref, w_ref, out_ref, kvw, qbuf, bias, abuf, wbuf, acc,
-          send1, recv1, send2, recv2, send3, recv3, send4,
+          send1, recv1, send2, recv2, send3, recv3, far3, send4,
           ky_s, ky_r, kz_s, kz_r, sw_s, sw_r, q_s, q_r, own_w, w_s, w_r, a_s, a_r,
           s1, r1, s2, r2, s3, r3, s4, r4):
     head, heads, kvh, hp, hpp, halves, lanes, pairs, cw = plan
@@ -26,13 +27,38 @@
     own_chunks = w_ref.shape[1] // cw
     chunks = own_chunks * pairs
     items = lanes * pairs * chunks
-    early = EARLY * pairs * own_chunks
+    soon = own_chunks // 2
+    segments = [(0, 2, 0, own_chunks), (0, 2, own_chunks, soon), (2, 1, 0, own_chunks + soon),
+                (0, EARLY, own_chunks + soon, own_chunks - soon),
+                (EARLY, lanes - EARLY, 0, chunks)]
+    starts = [0]
+    for _, planes, _, some in segments:
+        starts.append(starts[-1] + planes * pairs * some)
+    places = {}
+    for (k0, planes, c0, some), n0 in zip(segments[:-1], starts):
+        for r in range(planes * pairs * some):
+            places[k0 + r // (pairs * some), r // some % pairs, c0 + r % some] = n0 + r
+    swapped = (lanes - EARLY) * pairs * chunks
+    ordered = [c for c in range(chunks) if c % own_chunks >= soon]
+    ordered = ordered + [c for c in range(chunks) if c not in ordered]
+    partner = [(c + own_chunks) % chunks for c in ordered]
+    last = [[(k, c) for k in range(EARLY) for c in range(chunks) if (c % own_chunks < soon) == kind]
+            for kind in (True, False)]
+    settle = [
+        max([max(places[k, 1, c], places[k, 0, (c + own_chunks) % chunks]) + LAG + 1 - m
+             for m, (k, c) in enumerate(some)] + [starts[3] + 2])
+        for some in last
+    ]
+    settle.append(settle[1] + swapped)
+    settle[1] = max(settle[1], settle[0] + len(last[0]))
+    settle[2] = max(settle[2], settle[0] + len(last[0]))
     back = REACH // pairs
-    half_pieces = hp // hpp
-    pieces = half_pieces * pairs
+    pieces = hp // hpp * pairs
     piece = hpp * head
-    lag = min(4, pieces)
     per_kv = hp // kvh
+    per_run = per_kv // hpp
+    each = -(-pieces // 3)
+    wait_for = own_chunks * pairs - 1 if own_chunks > 1 else 0
     part = tokens // lanes
     a, g, s = lax.axis_index("grp"), lax.axis_index("kv"), lax.axis_index("srv")
     u, v = s // pairs, s % pairs
@@ -127,6 +153,7 @@
     for j in range(kvh):
         kv_beside(j).start()
         pl.when(right)(lambda j=j: kv_up(1, 0, j).start())
+    for j in range(kvh):
         query(j).start()
     for c in range(own_chunks):
         weight(c).start()
@@ -157,18 +184,21 @@
             allowed = (key_pos >= first) & (key_pos <= query_pos)
             bias[h, :, d * tokens:(d + 1) * tokens] = jnp.where(allowed, 0.0, FAR)
 
+    def kv_hop(d, j):
+        @pl.when(u >= d)
+        def _():
+            for w in range(pairs):
+                kv_up(d, w, j).wait_recv()
+                if d < back:
+                    pl.when(right)(lambda w=w: kv_up(d + 1, w, j).start())
+                swap(d, w, j, a).start()
+
     def kv_phase(j):
         kv_came(j).wait_recv()
         pl.when(right)(lambda: kv_up(1, 1, j).start())
         swap(0, 1, j, a).start()
-        for d in range(1, back + 1):
-            @pl.when(u >= d)
-            def _():
-                for w in range(pairs):
-                    kv_up(d, w, j).wait_recv()
-                    if d < back:
-                        pl.when(right)(lambda w=w: kv_up(d + 1, w, j).start())
-                    swap(d, w, j, a).start()
+        for d in range(1, back):
+            kv_hop(d, j)
 
     def kv_ready(j):
         swap(0, 1, j, 1 - a).wait_recv()
@@ -178,8 +208,15 @@
                 for w in range(pairs):
                     swap(d, w, j, 1 - a).wait_recv()
 
+    def run(b):
+        other = (b >= 1) & (b <= kvh)
+        h = jnp.where(other, 0, 1)
+        j = jnp.where(b <= 1, 0, jnp.where(other, b - 1, b - kvh))
+        return h, j
+
     def bit(p, i):
-        h, r = i // half_pieces, i % half_pieces
+        h, j = run(i // per_run)
+        r = j * per_run + i % per_run
         return abuf.at[p, jnp.where(h == 0, ov, v), :, lane_at(r * piece, piece)]
 
     def relay(way, d, i):
@@ -206,19 +243,24 @@
                 relay(way, d, i).start()
 
     factor = math.log2(math.e) / math.sqrt(head)
-    kv_phase(0)
+    for j in range(min(2, kvh)):
+        kv_phase(j)
+    kv_hop(back, 0)
     kv_ready(0)
 
-    def per_unit(i, carry):
-        h, hh = i // hp, i % hp
+    def per_unit(i):
+        h, kj = run(i // per_kv)
+        hh = kj * per_kv + i % per_kv
         vv = jnp.where(h == 0, ov, v)
         for j in range(kvh):
             if j > 0:
-                pl.when(i == (j - 1) * per_kv + min(2, per_kv - 1))(lambda: kv_phase(j))
-                pl.when(i == j * per_kv)(lambda: kv_ready(j))
-            pl.when(i == j * per_kv)(lambda: query(j).wait_recv())
+                if j > 1:
+                    pl.when(i == (j - 1) * per_kv)(lambda: kv_phase(j))
+                pl.when(i == (j + 1) * per_kv - 1)(lambda: kv_hop(back, j))
+                pl.when(i == (j + 1) * per_kv)(lambda: kv_ready(j))
+            pl.when(i == (j + 1) * per_kv)(lambda: query(j).wait_recv())
         mine = lane_at(hh * head, head)
-        at = lane_at((hh // heads) * head, head)
+        at = lane_at(kj * head, head)
         window = kvw[0, pl.ds(vv, REACH + 1), :, at].reshape((REACH + 1) * tokens, head)
         scores = lax.dot_general(
             qbuf[h, :, mine], window, (((1,), (1,)), ((), ())),
@@ -239,11 +281,9 @@
             n = i // hpp
             for way in range(2):
                 pl.when(may_send(way))(lambda: relay(way, 1, n).start())
-            pl.when(n >= lag)(lambda: forward(2, n - lag))
-
-        return carry
-
-    lax.fori_loop(0, hp * pairs, per_unit, 0)
+
+    units = hp * pairs
+    ahead_by = units - own_chunks - 1
 
     def plane(k):
         low = jnp.minimum(u, lanes - 1 - u)
@@ -251,18 +291,33 @@
         line = jnp.where(u < lanes - 1 - u, k, lanes - 1 - k)
         return jnp.where(k <= 2 * low, zigzag, line)
 
+    inside = left & right
+
+    def pick(i, values):
+        found = jnp.int32(values[0])
+        for at, value in enumerate(values[1:], 1):
+            found = jnp.where(i == at, value, found)
+        return found
+
     def decode(n):
-        m = n - early
-        r = n - EARLY * pairs * chunks
-        late = n >= EARLY * pairs * chunks
-        first = n < early
-        k = jnp.where(first, n // (pairs * own_chunks),
-                      jnp.where(late, EARLY + r // (pairs * chunks), m % (pairs * EARLY) // pairs))
-        h = jnp.where(first, n // own_chunks % pairs,
-                      jnp.where(late, r // chunks % pairs, m % pairs))
-        c = jnp.where(first, n % own_chunks,
-                      jnp.where(late, r % chunks, own_chunks + m // (pairs * EARLY)))
-        return k, h, c
+        k, h, c = jnp.int32(0), jnp.int32(0), jnp.int32(0)
+        fresh = jnp.bool_(False)
+        kept_in = n < items
+        m = jnp.where(n < starts[3] + swapped, n + starts[4] - starts[3], n - swapped)
+        n = jnp.where(inside & (n >= starts[3]) & (n < items), m, n)
+        for (k0, planes, c0, some), n0 in zip(segments, starts):
+            if planes * some == 0:
+                continue
+            r = n - n0
+            here = r >= 0
+            half, order = r // some % pairs, c0 + r % some
+            if k0 == EARLY:
+                order = jnp.where(half == 0, pick(r % some, ordered), pick(r % some, partner))
+            k = jnp.where(here, k0 + r // (pairs * some), k)
+            h = jnp.where(here, half, h)
+            c = jnp.where(here, order, c)
+            fresh = jnp.where(here, (r % some == 0) & (c0 == 0), fresh)
+        return k, h, c, fresh & (k > 0) & kept_in
 
     def column(c):
         return jnp.where(c < own_chunks, v * own_chunks + c, ov * own_chunks + c - own_chunks)
@@ -293,7 +348,7 @@
         return remote(send4.at[0, c], result(p, c), s4.at[0, c], r4.at[p, c], giver(p))
 
     def stage1(n):
-        k, h, c = decode(n)
+        k, h, c, _ = decode(n)
         product = jnp.dot(abuf[plane(k), jnp.where(h == 0, ov, v)], wbuf[c],
                           preferred_element_type=jnp.float32)
         low, high = product[:tokens // 2], product[tokens // 2:]
@@ -301,40 +356,76 @@
         send1[n] = jnp.where(a == 0, high, low).astype(send1.dtype)
         to_core(n).start()
 
-    def stage2(n):
-        to_core(n).wait_recv()
-        total = acc[n] + recv1[n].astype(jnp.float32)
+    def far_beside(k, c, n):
+        return remote(send2.at[n], far3.at[k - EARLY, c], s3.at[k, c], r3.at[k, c], beside)
+
+    def to_halves(n, total):
         acc[n] = total
         send2[n] = total.astype(send2.dtype)
         for k in range(1, halves):
             to_half(n, k).start()
 
+    def direct(k, c):
+        return (k >= EARLY) & (c % own_chunks >= soon)
+
+    def stage2(n):
+        k, h, c, _ = decode(n)
+        col = column(c)
+        to_core(n).wait_recv()
+        total = acc[n] + recv1[n].astype(jnp.float32)
+        y_first = direct(k, c)
+        pl.when(jnp.logical_not(y_first))(lambda: to_halves(n, total))
+
+        @pl.when(y_first & (h == 0))
+        def _():
+            send2[n] = total.astype(send2.dtype)
+            far_beside(k, col, n).start()
+
+        @pl.when(y_first & (h != 0))
+        def _():
+            far_beside(k, col, n).wait_recv()
+            to_halves(n, total + far3[k - EARLY, col].astype(jnp.float32))
+
     kept = pl.ds(g * part, part)
 
+    def deliver(k, col, total):
+        send4[k, col] = total.astype(send4.dtype)
+        pl.when(at_home & (k == 0))(lambda: to_self(col).start())
+        pl.when(jnp.logical_not(at_home & (k == 0)))(lambda: to_owner(k, col).start())
+
     def stage3(n):
-        k, h, c = decode(n)
-        if halves > 1:
+        k, h, c, _ = decode(n)
+        col = column(c)
+
+        y_first = direct(k, c)
+
+        @pl.when(jnp.logical_not(y_first) | (h != 0))
+        def _():
             all_halves(n).wait_recv()
-        total = acc[n, kept]
-        for i in range(halves - 1):
-            total = total + recv2[n, i].astype(jnp.float32)
-
-        @pl.when(h == 0)
-        def _():
-            send3[k, column(c)] = total.astype(send3.dtype)
-            to_beside(k, column(c)).start()
-
-        @pl.when(h != 0)
-        def _():
-            acc[n, kept] = total
+            total = acc[n, kept]
+            for i in range(halves - 1):
+                total = total + recv2[n, i].astype(jnp.float32)
+
+            @pl.when(h == 0)
+            def _():
+                send3[k, col] = total.astype(send3.dtype)
+                to_beside(k, col).start()
+
+            @pl.when((h != 0) & (k < EARLY))
+            def _():
+                acc[n, kept] = total
+
+            pl.when((h != 0) & y_first)(lambda: deliver(k, col, total))
+
+            @pl.when((h != 0) & (k >= EARLY) & jnp.logical_not(y_first))
+            def _():
+                to_beside(k, col).wait_recv()
+                deliver(k, col, total + recv3[k, col].astype(jnp.float32))
 
     def stage4(n, k, c):
         col = column(c)
         to_beside(k, col).wait_recv()
-        total = acc[n, kept] + recv3[k, col].astype(jnp.float32)
-        send4[k, col] = total.astype(send4.dtype)
-        pl.when(at_home & (k == 0))(lambda: to_self(col).start())
-        pl.when(jnp.logical_not(at_home & (k == 0)))(lambda: to_owner(k, col).start())
+        deliver(k, col, acc[n, kept] + recv3[k, col].astype(jnp.float32))
 
     def arrived(k, h):
         p = plane(k)
@@ -345,22 +436,30 @@
         @pl.when(jnp.logical_not(jnp.where(up, right, left)))
         def _():
             def one(r, carry):
-                i = h * half_pieces + r
+                i = jnp.where(h == 0, per_run + r,
+                              jnp.where(r < per_run, r, r + kvh * per_run))
                 remote(bit(p, i), bit(p, i), a_s.at[way, d - 1, i], a_r.at[way, d - 1, i],
                        core).wait_recv()
                 return carry
 
-            lax.fori_loop(0, half_pieces, one, 0)
-
-    first_end = EARLY * chunks
-
-    def per_item(n, carry):
-        k, h, c = decode(n)
-        pl.when(n < lag)(lambda: forward(2, pieces - lag + n))
+            lax.fori_loop(0, kvh * per_run, one, 0)
+
+    def per_item(n):
+        k, h, c, fresh = decode(n)
+
+        f = (n - wait_for) * each
+
+        @pl.when((f >= 0) & (f < pieces))
+        def _():
+            for i in range(each):
+                pl.when(f + i < pieces)(lambda i=i: forward(2, f + i))
+
         if lanes > 3:
-            pl.when((n >= lag) & (n < lag + pieces))(lambda: forward(3, n - lag))
+            for i in range(pieces):
+                at = starts[1] + (starts[3] - starts[1] + 1) * i // pieces
+                pl.when(n == at)(lambda i=i: forward(3, i))
         if lanes > 4:
-            @pl.when(n == lag + pieces)
+            @pl.when(n == starts[3])
             def _():
                 for d in range(4, lanes):
                     def one(i, carry):
@@ -370,9 +469,11 @@
                     lax.fori_loop(0, pieces, one, 0)
 
         for i in range(own_chunks):
+            used = starts[1] + i if i < soon else starts[3]
             pl.when(n == i)(lambda i=i: own_weight(i).wait())
-            pl.when(n == early + i * pairs * EARLY)(lambda i=i: weight(i).wait_recv())
-        fresh = (n < items) & (c == 0) & (k > 0) & (h < pairs)
+            pl.when(n == used)(lambda i=i: weight(i).wait_recv())
+        done = decode(n - 1)[3]
+        pl.when(fresh & jnp.logical_not(done) & (n >= 2))(lambda: stage2(n - 2))
 
         @pl.when(fresh)
         def _():
@@ -380,22 +481,26 @@
             arrived(k, h)
 
         pl.when(n < items)(lambda: stage1(n))
-        pl.when(jnp.logical_not(fresh) & (n >= 1) & (n <= items))(lambda: stage2(n - 1))
-        pl.when((n >= 3) & (n < items + 3))(lambda: stage3(n - 3))
-        m = n - (first_end + EARLY * own_chunks + 2)
-
-        @pl.when((m >= 0) & (m < first_end))
-        def _():
-            mk, mc = m // chunks, m % chunks
-            index = jnp.where(mc < own_chunks, mk * pairs * own_chunks + own_chunks + mc,
-                              early + (mc - own_chunks) * pairs * EARLY + mk * pairs + 1)
-            stage4(index, mk, mc)
-
-        lk, lh, lc = decode(n - 4)
-        pl.when((n - 4 >= EARLY * pairs * chunks) & (lh == 1))(lambda: stage4(n - 4, lk, lc))
+        pending = jnp.logical_not(fresh | done) & (n >= 2) & (n < items + 2)
+        pl.when(pending)(lambda: stage2(n - 2))
+        pl.when((n >= LAG) & (n < items + LAG))(lambda: stage3(n - LAG))
+        later = jnp.where(inside, swapped, 0)
+        index, mk, mc = jnp.int32(-1), jnp.int32(0), jnp.int32(0)
+        begins = settle[0], jnp.where(inside, settle[2], settle[1])
+        for some, first, shift in zip(last, begins, (0, later)):
+            for m, (k1, c1) in enumerate(some):
+                here = n == first + m
+                held = places[k1, 1, c1]
+                index = jnp.where(here, held + (shift if held >= starts[3] else 0), index)
+                mk, mc = jnp.where(here, k1, mk), jnp.where(here, c1, mc)
+        pl.when(index >= 0)(lambda: stage4(index, mk, mc))
+
+    def step(i, carry):
+        pl.when(i < units)(lambda: per_unit(i))
+        pl.when(i >= ahead_by)(lambda: per_item(i - ahead_by))
         return carry
 
-    lax.fori_loop(0, items + 4, per_item, 0)
+    lax.fori_loop(0, ahead_by + max(items + LAG, settle[2] + len(last[1])), step, 0)
 
     for j in range(kvh):
         kv_beside(j).wait_send()
@@ -418,16 +523,19 @@
                 lax.fori_loop(0, pieces, one, 0)
 
     def sent(n, carry):
+        k, h, c, _ = decode(n)
         to_core(n).wait_send()
-        if halves > 1:
-            all_halves(n).wait_send()
+        near = jnp.logical_not(direct(k, c)) | (h != 0)
+        pl.when(near)(lambda: all_halves(n).wait_send())
+        pl.when(jnp.logical_not(near))(lambda: far_beside(k, column(c), n).wait_send())
         return carry
 
     lax.fori_loop(0, items, sent, 0)
 
     def finish(i, carry):
         k, c = i // chunks, i % chunks
-        to_beside(k, c).wait_send()
+        y_first = (k >= EARLY) & (c % own_chunks >= soon)
+        pl.when(jnp.logical_not(y_first))(lambda: to_beside(k, c).wait_send())
         pl.when(jnp.logical_not(at_home & (k == 0)))(lambda: to_owner(k, c).wait_send())
         pl.when(at_home & (k == q))(lambda: to_self(c).wait())
         pl.when(jnp.logical_not(at_home & (k == q)))(lambda: given(k, c).wait_recv())
@@ -441,7 +549,7 @@
     cores, halves = lax.axis_size("grp"), lax.axis_size("kv")
     lanes = cores * halves
     pairs = lax.axis_size("srv") // lanes
-    assert cores == 2 and pairs == 2 and lanes > 2
+    assert cores == 2 and pairs == 2 and halves > 1 and lanes > EARLY
     q = queries.reshape(tokens, -1)
     kv = jnp.stack([keys.reshape(tokens, -1), values.reshape(tokens, -1)])
     groups, head = keys.shape[1], keys.shape[2]
@@ -484,6 +592,7 @@
             pltpu.VMEM((items, halves - 1, part, cw), bf16),
             pltpu.VMEM((lanes, chunks, part, cw), bf16),
             pltpu.VMEM((lanes, chunks, part, cw), bf16),
+            pltpu.VMEM((lanes - EARLY, chunks, tokens // cores, cw), bf16),
             pltpu.VMEM((lanes, chunks, part, cw), bf16),
             dma((kvh,)), dma((kvh,)), dma((back, pairs, kvh)), dma((back, pairs, kvh)),
             dma((2 * back + 1, kvh)), dma((2 * back + 1, kvh)), dma((kvh,)), dma((kvh,)),

time: 138 us -> 125 us (0.906)
  the two profiles are of different devices: /device:TPU:5 before, /device:TPU:3 now
where the time goes in v2:
time: 125 us; the launch traced here: 124 us
  Pallas kernels  117 us (94%)
  local copies, waits for them, and re-layouts  6.88 us (6%)
    pallas_call x1, Pallas kernels, on_device(): pl.pallas_call(functools.partial(layer, (head, heads, kvh, hp, hpp, halve...  117 us
    unnamed x2, local copies, waits for them, and re-layouts  4.78 us

profile of v2, /device:TPU:3, one launch (start us, length us, event | category | flops | bytes accessed | tf_op | source)
XLA Modules:
  0.0 124.3 jit_solution(7509360419945422696)
XLA Ops:
  0.0 1.1 stack_reshape.6
  1.1 1.1 stack_reshape.7
  2.1 0.9 pad_maximum_fusion.kv_ref
  3.0 2.5 %copy.6 = bf16[32,8,4,512]{3,1,2,0:T(8,128)(2,1)} copy(bf16[32,8,4,512]{3,2,1,0:T(4,128)(2,1)} %bitcast.5) | data formatting | bytes 2097152
  5.4 116.5 %shard_map.55 = bf16[256,2048]{1,0:T(8,128)(2,1)} custom-call(s32[4]{0:T(128)} %lengths.1, bf16[256,2048]{1,0:T(8,128)(2,1)} %bitcast.4, bf16[2,256,512]{2,1,0:T(8,128)(2,1)} %pad_maximum_fusion.kv_ref, bf16[2048,1024]{1,0:T(8,128)(2,1)} %bitcast.3), custom_call_target="tpu_custom_call" | custom-call | tf_op jit(solution)/shard_map/pallas_call | solution.py:574
  122.0 2.3 %copy.8 = bf16[256,2048]{1,0:T(8,128)(2,1)} copy(bf16[256,2048]{1,0:T(8,128)(2,1)} %shard_map.55) | data formatting | bytes 2097152

commit v3 on v2

--- a/solution.py
+++ b/solution.py
@@ -15,10 +15,11 @@
 MESH = pl.DeviceIdType.MESH
 
 
-def layer(plan, lengths, q_ref, kv_ref, w_ref, out_ref, kvw, qbuf, bias, abuf, wbuf, acc,
+def layer(plan, lengths_in, q_hbm, k_hbm, v_hbm, w_ref, out_ref,
+          lengths, q_in, k_in, v_in, q_ref, kv_ref, kvw, qbuf, bias, abuf, wbuf, acc,
           send1, recv1, send2, recv2, send3, recv3, far3, send4,
           ky_s, ky_r, kz_s, kz_r, sw_s, sw_r, q_s, q_r, own_w, w_s, w_r, a_s, a_r,
-          s1, r1, s2, r2, s3, r3, s4, r4):
+          s1, r1, s2, r2, s3, r3, s4, r4, in_s):
     head, heads, kvh, hp, hpp, halves, lanes, pairs, cw = plan
     tokens = q_ref.shape[0]
     inner = hp * head
@@ -81,6 +82,14 @@
     def giver(p):
         return (p // halves, p % halves, q * pairs + v)
 
+    arriving = [
+        pltpu.make_async_copy(src, dst, in_s.at[i])
+        for i, (src, dst) in enumerate(
+            ((k_hbm, k_in), (v_hbm, v_in), (q_hbm, q_in), (lengths_in, lengths)))
+    ]
+    for copy in arriving:
+        copy.start()
+
     barrier = pltpu.get_barrier_semaphore()
 
     def greet(device):
@@ -148,11 +157,21 @@
     for c in range(own_chunks):
         own_weight(c).start()
 
+    arriving[0].wait()
+    arriving[1].wait()
+    for j in range(k_in.shape[1]):
+        kv_ref[0, :, j * head:(j + 1) * head] = k_in[:, j]
+        kv_ref[1, :, j * head:(j + 1) * head] = v_in[:, j]
+
     pl.semaphore_wait(barrier, peers)
 
     for j in range(kvh):
         kv_beside(j).start()
         pl.when(right)(lambda j=j: kv_up(1, 0, j).start())
+    span = q_in.shape[2]
+    arriving[2].wait()
+    for j in range(q_in.shape[1]):
+        q_ref[:, j * span:(j + 1) * span] = q_in[:, j]
     for j in range(kvh):
         query(j).start()
     for c in range(own_chunks):
@@ -169,6 +188,7 @@
                 for w in range(pairs):
                     kvw[m, (back - d) * pairs + w] = jnp.zeros((tokens, width), kvw.dtype)
 
+    arriving[3].wait()
     row = lax.broadcasted_iota(jnp.int32, (tokens, 1), 0)
     lane = lax.broadcasted_iota(jnp.int32, (tokens, tokens), 1)
     for h in range(pairs):
@@ -550,10 +570,8 @@
     lanes = cores * halves
     pairs = lax.axis_size("srv") // lanes
     assert cores == 2 and pairs == 2 and halves > 1 and lanes > EARLY
-    q = queries.reshape(tokens, -1)
-    kv = jnp.stack([keys.reshape(tokens, -1), values.reshape(tokens, -1)])
     groups, head = keys.shape[1], keys.shape[2]
-    inner = q.shape[1]
+    inner = groups * queries.shape[2]
     weight = output_projection_weight.reshape(inner, -1)
     columns = weight.shape[1]
     heads = inner // (groups * head)
@@ -570,16 +588,19 @@
     width = kvh * head
     dma = pltpu.SemaphoreType.DMA
     bf16, f32 = jnp.bfloat16, jnp.float32
-    vmem = pl.BlockSpec(memory_space=pltpu.VMEM)
+    hbm = pl.BlockSpec(memory_space=pltpu.HBM)
     return pl.pallas_call(
         functools.partial(layer, (head, heads, kvh, hp, hpp, halves, lanes, pairs, cw)),
         out_shape=jax.ShapeDtypeStruct((tokens, pairs * columns), bf16),
-        in_specs=[
-            pl.BlockSpec(memory_space=pltpu.SMEM), vmem, vmem,
-            pl.BlockSpec(memory_space=pl.ANY),
-        ],
+        in_specs=[hbm] * 5,
         out_specs=pl.BlockSpec(memory_space=pl.ANY),
         scratch_shapes=[
+            pltpu.SMEM(lengths.shape, lengths.dtype),
+            pltpu.VMEM(queries.shape, bf16),
+            pltpu.VMEM(keys.shape, bf16),
+            pltpu.VMEM(values.shape, bf16),
+            pltpu.VMEM((tokens, inner), bf16),
+            pltpu.VMEM((2, tokens, groups * head), bf16),
             pltpu.VMEM((2, (back + 1) * pairs, tokens, width), bf16),
             pltpu.VMEM((pairs, tokens, hp * head), bf16),
             pltpu.VMEM((pairs, tokens, (REACH + 1) * tokens), f32),
@@ -600,11 +621,12 @@
             dma((2, lanes - 1, pieces)), dma((2, lanes - 1, pieces)),
             dma((items,)), dma((items,)), dma((items,)), dma((items,)),
             dma((lanes, chunks)), dma((lanes, chunks)), dma((lanes, chunks)), dma((lanes, chunks)),
+            dma((4,)),
         ],
         compiler_params=pltpu.CompilerParams(
-            collective_id=0, has_side_effects=True, vmem_limit_bytes=60 * 1024 * 1024
+            collective_id=0, has_side_effects=True, vmem_limit_bytes=52 * 1024 * 1024
         ),
-    )(lengths, q, kv, weight)
+    )(*[pltpu.with_memory_space_constraint(x, pltpu.HBM) for x in (lengths, queries, keys, values, weight)])
 
 
 def solution(mesh):

time: 125 us -> 116 us (0.928)
  local copies, waits for them, and re-layouts: 6.88 us -> 0.97 us
  Pallas kernels: 117 us -> 115 us
    unnamed x2 -> x1, local copies, waits for them, and re-layouts: 4.78 us -> 0.97 us
    another operation x2 -> x0, local copies, waits for them, and re-layouts: 2.1 us -> none  [on_device(): kv = jnp.stack([keys.reshape(tokens, -1), values.reshape(tokens, -1)])]
    pallas_call x1, Pallas kernels: 117 us -> 115 us  [on_device(): pl.pallas_call(functools.partial(layer, (head, heads, kvh, hp, hpp, halve...]
where the time goes in v3:
time: 116 us
  Pallas kernels  115 us (99%)
    pallas_call x1, Pallas kernels, on_device(): pl.pallas_call(functools.partial(layer, (head, heads, kvh, hp, hpp, halve...  115 us

profile of v3, /device:TPU:3, one launch (start us, length us, event | category | flops | bytes accessed | tf_op | source)
XLA Modules:
  0.0 116.0 jit_solution(13807796358871994843)
XLA Ops:
  0.0 115.0 %shard_map.55 = bf16[256,2048]{1,0:T(8,128)(2,1)S(1)} custom-call(s32[4]{0:T(128)} %lengths_in.1, bf16[256,4,512]{2,1,0:T(4,128)(2,1)} %q_hbm.1, bf16[256,4,128]{2,1,0:T(4,128)(2,1)} %k_hbm.1, bf16[256,4,128]{2,1,0:T(4,128)(2,1)} %v_hbm.1, bf16[2048,1024]{1,0:T(8,128)(2,1)} %bitcast.1), custom_call_target="tpu_custom_call" | custom-call | tf_op jit(solution)/shard_map/pallas_call | solution.py:592
  115.0 1.0 copy.7

commit v4 on v3

--- a/solution.py
+++ b/solution.py
@@ -59,7 +59,7 @@
     per_kv = hp // kvh
     per_run = per_kv // hpp
     each = -(-pieces // 3)
-    wait_for = own_chunks * pairs - 1 if own_chunks > 1 else 0
+    wait_for = own_chunks * pairs - 1
     part = tokens // lanes
     a, g, s = lax.axis_index("grp"), lax.axis_index("kv"), lax.axis_index("srv")
     u, v = s // pairs, s % pairs
@@ -229,10 +229,7 @@
                     swap(d, w, j, 1 - a).wait_recv()
 
     def run(b):
-        other = (b >= 1) & (b <= kvh)
-        h = jnp.where(other, 0, 1)
-        j = jnp.where(b <= 1, 0, jnp.where(other, b - 1, b - kvh))
-        return h, j
+        return b // kvh, b % kvh
 
     def bit(p, i):
         h, j = run(i // per_run)
@@ -241,12 +238,12 @@
 
     def relay(way, d, i):
         p = u - (d - 1) if way == 0 else u + (d - 1)
-        return remote(bit(p, i), bit(p, i), a_s.at[way, d - 1, i], a_r.at[way, d - 1, i],
+        return remote(bit(p, i), bit(p, i), a_s.at[way, d - 1], a_r.at[way, d - 1, i],
                       ahead if way == 0 else behind)
 
     def relayed(way, d, i):
         p = u - d if way == 0 else u + d
-        return remote(bit(p, i), bit(p, i), a_s.at[way, d - 1, i], a_r.at[way, d - 1, i],
+        return remote(bit(p, i), bit(p, i), a_s.at[way, d - 1], a_r.at[way, d - 1, i],
                       behind if way == 0 else ahead)
 
     def holds(way, d):
@@ -276,9 +273,9 @@
             if j > 0:
                 if j > 1:
                     pl.when(i == (j - 1) * per_kv)(lambda: kv_phase(j))
-                pl.when(i == (j + 1) * per_kv - 1)(lambda: kv_hop(back, j))
-                pl.when(i == (j + 1) * per_kv)(lambda: kv_ready(j))
-            pl.when(i == (j + 1) * per_kv)(lambda: query(j).wait_recv())
+                pl.when(i == j * per_kv - 1)(lambda: kv_hop(back, j))
+                pl.when(i == j * per_kv)(lambda: kv_ready(j))
+            pl.when(i == j * per_kv)(lambda: query(j).wait_recv())
         mine = lane_at(hh * head, head)
         at = lane_at(kj * head, head)
         window = kvw[0, pl.ds(vv, REACH + 1), :, at].reshape((REACH + 1) * tokens, head)
@@ -343,29 +340,27 @@
         return jnp.where(c < own_chunks, v * own_chunks + c, ov * own_chunks + c - own_chunks)
 
     def to_core(n):
-        return remote(send1.at[n], recv1.at[n], s1.at[n], r1.at[n], core)
+        return remote(send1.at[n], recv1.at[n], s1.at[0], r1.at[n], core)
 
     def to_half(n, k):
         rows = pl.ds((g + k) % halves * part, part)
-        return remote(send2.at[n, rows], recv2.at[n, k - 1], s2.at[n], r2.at[n], other_half(k))
+        return remote(send2.at[n, rows], recv2.at[n, k - 1], s2.at[0], r2.at[n], other_half(k))
 
     def all_halves(n):
-        return remote(recv2.at[n], recv2.at[n], s2.at[n], r2.at[n], other_half(1))
+        return remote(recv2.at[n], recv2.at[n], s2.at[0], r2.at[n], other_half(1))
 
     def to_beside(k, c):
-        return remote(send3.at[k, c], recv3.at[k, c], s3.at[k, c], r3.at[k, c], beside)
+        i = k * chunks + c
+        return remote(send3.at[i], recv3.at[i], s3.at[0], r3.at[i], beside)
 
     def result(giver_index, c):
         return out_ref.at[pl.ds(giver_index * part, part), lane_at(c * cw, cw)]
 
     def to_owner(k, c):
-        return remote(send4.at[k, c], result(q, c), s4.at[k, c], r4.at[q, c], owner(plane(k)))
+        return remote(send4.at[k * chunks + c], result(q, c), s4.at[0], r4.at[0], owner(plane(k)))
 
     def to_self(c):
-        return pltpu.make_async_copy(send4.at[0, c], result(q, c), r4.at[q, c])
-
-    def given(p, c):
-        return remote(send4.at[0, c], result(p, c), s4.at[0, c], r4.at[p, c], giver(p))
+        return pltpu.make_async_copy(send4.at[c], result(q, c), r4.at[0])
 
     def stage1(n):
         k, h, c, _ = decode(n)
@@ -377,7 +372,8 @@
         to_core(n).start()
 
     def far_beside(k, c, n):
-        return remote(send2.at[n], far3.at[k - EARLY, c], s3.at[k, c], r3.at[k, c], beside)
+        return remote(send2.at[n], far3.at[(k - EARLY) * chunks + c], s3.at[1],
+                      r3.at[k * chunks + c], beside)
 
     def to_halves(n, total):
         acc[n] = total
@@ -404,12 +400,12 @@
         @pl.when(y_first & (h != 0))
         def _():
             far_beside(k, col, n).wait_recv()
-            to_halves(n, total + far3[k - EARLY, col].astype(jnp.float32))
+            to_halves(n, total + far3[(k - EARLY) * chunks + col].astype(jnp.float32))
 
     kept = pl.ds(g * part, part)
 
     def deliver(k, col, total):
-        send4[k, col] = total.astype(send4.dtype)
+        send4[k * chunks + col] = total.astype(send4.dtype)
         pl.when(at_home & (k == 0))(lambda: to_self(col).start())
         pl.when(jnp.logical_not(at_home & (k == 0)))(lambda: to_owner(k, col).start())
 
@@ -428,7 +424,7 @@
 
             @pl.when(h == 0)
             def _():
-                send3[k, col] = total.astype(send3.dtype)
+                send3[k * chunks + col] = total.astype(send3.dtype)
                 to_beside(k, col).start()
 
             @pl.when((h != 0) & (k < EARLY))
@@ -440,12 +436,12 @@
             @pl.when((h != 0) & (k >= EARLY) & jnp.logical_not(y_first))
             def _():
                 to_beside(k, col).wait_recv()
-                deliver(k, col, total + recv3[k, col].astype(jnp.float32))
+                deliver(k, col, total + recv3[k * chunks + col].astype(jnp.float32))
 
     def stage4(n, k, c):
         col = column(c)
         to_beside(k, col).wait_recv()
-        deliver(k, col, acc[n, kept] + recv3[k, col].astype(jnp.float32))
+        deliver(k, col, acc[n, kept] + recv3[k * chunks + col].astype(jnp.float32))
 
     def arrived(k, h):
         p = plane(k)
@@ -456,9 +452,8 @@
         @pl.when(jnp.logical_not(jnp.where(up, right, left)))
         def _():
             def one(r, carry):
-                i = jnp.where(h == 0, per_run + r,
-                              jnp.where(r < per_run, r, r + kvh * per_run))
-                remote(bit(p, i), bit(p, i), a_s.at[way, d - 1, i], a_r.at[way, d - 1, i],
+                i = h * kvh * per_run + r
+                remote(bit(p, i), bit(p, i), a_s.at[way, d - 1], a_r.at[way, d - 1, i],
                        core).wait_recv()
                 return carry
 
@@ -490,7 +485,6 @@
 
         for i in range(own_chunks):
             used = starts[1] + i if i < soon else starts[3]
-            pl.when(n == i)(lambda i=i: own_weight(i).wait())
             pl.when(n == used)(lambda i=i: weight(i).wait_recv())
         done = decode(n - 1)[3]
         pl.when(fresh & jnp.logical_not(done) & (n >= 2))(lambda: stage2(n - 2))
@@ -501,7 +495,7 @@
             arrived(k, h)
 
         pl.when(n < items)(lambda: stage1(n))
-        pending = jnp.logical_not(fresh | done) & (n >= 2) & (n < items + 2)
+        pending = jnp.logical_not(fresh | done) & (n >= 2 + own_chunks) & (n < items + 2)
         pl.when(pending)(lambda: stage2(n - 2))
         pl.when((n >= LAG) & (n < items + LAG))(lambda: stage3(n - LAG))
         later = jnp.where(inside, swapped, 0)
@@ -517,10 +511,22 @@
 
     def step(i, carry):
         pl.when(i < units)(lambda: per_unit(i))
-        pl.when(i >= ahead_by)(lambda: per_item(i - ahead_by))
+        for c in range(own_chunks):
+            @pl.when(i == hp + 2 * c)
+            def _():
+                own_weight(c).wait()
+                stage1(c)
+
+            pl.when(i == hp + 2 * c + 1)(lambda: stage2(c))
+        pl.when(i >= units - 1)(lambda: per_item(i - ahead_by))
         return carry
 
     lax.fori_loop(0, ahead_by + max(items + LAG, settle[2] + len(last[1])), step, 0)
+
+    far = (lanes - EARLY) * sum(c % own_chunks >= soon for c in range(chunks))
+
+    def sent(ref, sem):
+        remote(ref, ref, sem, sem, core).wait_send()
 
     for j in range(kvh):
         kv_beside(j).wait_send()
@@ -534,34 +540,17 @@
         weight(c).wait_send()
     for d in range(1, lanes):
         for way in range(2):
-            @pl.when(holds(way, d - 1) & may_send(way))
-            def _():
-                def one(i, carry):
-                    relay(way, d, i).wait_send()
-                    return carry
-
-                lax.fori_loop(0, pieces, one, 0)
-
-    def sent(n, carry):
-        k, h, c, _ = decode(n)
-        to_core(n).wait_send()
-        near = jnp.logical_not(direct(k, c)) | (h != 0)
-        pl.when(near)(lambda: all_halves(n).wait_send())
-        pl.when(jnp.logical_not(near))(lambda: far_beside(k, column(c), n).wait_send())
-        return carry
-
-    lax.fori_loop(0, items, sent, 0)
-
-    def finish(i, carry):
-        k, c = i // chunks, i % chunks
-        y_first = (k >= EARLY) & (c % own_chunks >= soon)
-        pl.when(jnp.logical_not(y_first))(lambda: to_beside(k, c).wait_send())
-        pl.when(jnp.logical_not(at_home & (k == 0)))(lambda: to_owner(k, c).wait_send())
-        pl.when(at_home & (k == q))(lambda: to_self(c).wait())
-        pl.when(jnp.logical_not(at_home & (k == q)))(lambda: given(k, c).wait_recv())
-        return carry
-
-    lax.fori_loop(0, lanes * chunks, finish, 0)
+            p = u - (d - 1) if way == 0 else u + (d - 1)
+            pl.when(holds(way, d - 1) & may_send(way))(
+                lambda p=p, way=way, d=d: sent(abuf.at[p], a_s.at[way, d - 1]))
+
+    sent(send1, s1.at[0])
+    sent(recv2.at[pl.ds(0, items - far)], s2.at[0])
+    sent(send3.at[pl.ds(0, lanes * chunks - far)], s3.at[0])
+    sent(far3.at[pl.ds(0, far)], s3.at[1])
+    pl.when(at_home)(lambda: sent(send4.at[pl.ds(chunks, (lanes - 1) * chunks)], s4.at[0]))
+    pl.when(jnp.logical_not(at_home))(lambda: sent(send4, s4.at[0]))
+    pltpu.make_async_copy(out_ref, out_ref, r4.at[0]).wait()
 
 
 def on_device(queries, keys, values, lengths, output_projection_weight):
@@ -611,16 +600,16 @@
             pltpu.VMEM((items, tokens // cores, cw), bf16),
             pltpu.VMEM((items, tokens // cores, cw), bf16),
             pltpu.VMEM((items, halves - 1, part, cw), bf16),
-            pltpu.VMEM((lanes, chunks, part, cw), bf16),
-            pltpu.VMEM((lanes, chunks, part, cw), bf16),
-            pltpu.VMEM((lanes - EARLY, chunks, tokens // cores, cw), bf16),
-            pltpu.VMEM((lanes, chunks, part, cw), bf16),
+            pltpu.VMEM((lanes * chunks, part, cw), bf16),
+            pltpu.VMEM((lanes * chunks, part, cw), bf16),
+            pltpu.VMEM(((lanes - EARLY) * chunks, tokens // cores, cw), bf16),
+            pltpu.VMEM((lanes * chunks, part, cw), bf16),
             dma((kvh,)), dma((kvh,)), dma((back, pairs, kvh)), dma((back, pairs, kvh)),
             dma((2 * back + 1, kvh)), dma((2 * back + 1, kvh)), dma((kvh,)), dma((kvh,)),
             dma((own_chunks,)), dma((own_chunks,)), dma((own_chunks,)),
-            dma((2, lanes - 1, pieces)), dma((2, lanes - 1, pieces)),
-            dma((items,)), dma((items,)), dma((items,)), dma((items,)),
-            dma((lanes, chunks)), dma((lanes, chunks)), dma((lanes, chunks)), dma((lanes, chunks)),
+            dma((2, lanes - 1)), dma((2, lanes - 1, pieces)),
+            dma((1,)), dma((items,)), dma((1,)), dma((items,)),
+            dma((2,)), dma((lanes * chunks,)), dma((1,)), dma((1,)),
             dma((4,)),
         ],
         compiler_params=pltpu.CompilerParams(

time: 116 us -> 115 us (level)
  no operation moved by 1% of the time
where the time goes in v4:
time: 115 us
  Pallas kernels  114 us (99%)
    pallas_call x1, Pallas kernels, on_device(): pl.pallas_call(functools.partial(layer, (head, heads, kvh, hp, hpp, halve...  114 us

profile of v4, /device:TPU:3, one launch (start us, length us, event | category | flops | bytes accessed | tf_op | source)
XLA Modules:
  0.0 115.0 jit_solution(17371390978095570275)
XLA Ops:
  0.0 114.0 %shard_map.55 = bf16[256,2048]{1,0:T(8,128)(2,1)S(1)} custom-call(s32[4]{0:T(128)} %lengths_in.1, bf16[256,4,512]{2,1,0:T(4,128)(2,1)} %q_hbm.1, bf16[256,4,128]{2,1,0:T(4,128)(2,1)} %k_hbm.1, bf16[256,4,128]{2,1,0:T(4,128)(2,1)} %v_hbm.1, bf16[2048,1024]{1,0:T(8,128)(2,1)} %bitcast.1), custom_call_target="tpu_custom_call" | custom-call | tf_op jit(solution)/shard_map/pallas_call | solution.py:581
  114.0 1.0 copy.7

commit v5 on v4

--- a/solution.py
+++ b/solution.py
@@ -12,6 +12,7 @@
 EARLY = 3
 FAR = -1e30
 LAG = 5
+RING = 8
 MESH = pl.DeviceIdType.MESH
 
 
@@ -340,14 +341,14 @@
         return jnp.where(c < own_chunks, v * own_chunks + c, ov * own_chunks + c - own_chunks)
 
     def to_core(n):
-        return remote(send1.at[n], recv1.at[n], s1.at[0], r1.at[n], core)
+        return remote(send1.at[n], recv1.at[n], s1.at[0], r1.at[n % RING], core)
 
     def to_half(n, k):
         rows = pl.ds((g + k) % halves * part, part)
-        return remote(send2.at[n, rows], recv2.at[n, k - 1], s2.at[0], r2.at[n], other_half(k))
+        return remote(send2.at[n, rows], recv2.at[n, k - 1], s2.at[0], r2.at[n % (2 * RING)], other_half(k))
 
     def all_halves(n):
-        return remote(recv2.at[n], recv2.at[n], s2.at[0], r2.at[n], other_half(1))
+        return remote(recv2.at[n], recv2.at[n], s2.at[0], r2.at[n % (2 * RING)], other_half(1))
 
     def to_beside(k, c):
         i = k * chunks + c
@@ -382,7 +383,7 @@
             to_half(n, k).start()
 
     def direct(k, c):
-        return (k >= EARLY) & (c % own_chunks >= soon)
+        return k >= EARLY
 
     def stage2(n):
         k, h, c, _ = decode(n)
@@ -523,7 +524,7 @@
 
     lax.fori_loop(0, ahead_by + max(items + LAG, settle[2] + len(last[1])), step, 0)
 
-    far = (lanes - EARLY) * sum(c % own_chunks >= soon for c in range(chunks))
+    far = (lanes - EARLY) * chunks
 
     def sent(ref, sem):
         remote(ref, ref, sem, sem, core).wait_send()
@@ -608,7 +609,7 @@
             dma((2 * back + 1, kvh)), dma((2 * back + 1, kvh)), dma((kvh,)), dma((kvh,)),
             dma((own_chunks,)), dma((own_chunks,)), dma((own_chunks,)),
             dma((2, lanes - 1)), dma((2, lanes - 1, pieces)),
-            dma((1,)), dma((items,)), dma((1,)), dma((items,)),
+            dma((1,)), dma((RING,)), dma((1,)), dma((2 * RING,)),
             dma((2,)), dma((lanes * chunks,)), dma((1,)), dma((1,)),
             dma((4,)),
         ],

time: 115 us -> 113 us (0.983); the launches traced: 115 us -> 112 us
  Pallas kernels: 114 us -> 111 us
    pallas_call x1, Pallas kernels: 114 us -> 111 us  [on_device(): pl.pallas_call(functools.partial(layer, (head, heads, kvh, hp, hpp, halve...]
where the time goes in v5:
time: 113 us; the launch traced here: 112 us
  Pallas kernels  111 us (98%)
    pallas_call x1, Pallas kernels, on_device(): pl.pallas_call(functools.partial(layer, (head, heads, kvh, hp, hpp, halve...  111 us

profile of v5, /device:TPU:3, one launch (start us, length us, event | category | flops | bytes accessed | tf_op | source)
XLA Modules:
  0.0 111.6 jit_solution(6083954035516017662)
XLA Ops:
  0.0 110.6 %shard_map.55 = bf16[256,2048]{1,0:T(8,128)(2,1)S(1)} custom-call(s32[4]{0:T(128)} %lengths_in.1, bf16[256,4,512]{2,1,0:T(4,128)(2,1)} %q_hbm.1, bf16[256,4,128]{2,1,0:T(4,128)(2,1)} %k_hbm.1, bf16[256,4,128]{2,1,0:T(4,128)(2,1)} %v_hbm.1, bf16[2048,1024]{1,0:T(8,128)(2,1)} %bitcast.1), custom_call_target="tpu_custom_call" | custom-call | tf_op jit(solution)/shard_map/pallas_call | solution.py:582
  110.6 1.0 copy.7

commit v6 on v5

--- a/solution.py
+++ b/solution.py
@@ -41,8 +41,7 @@
         for r in range(planes * pairs * some):
             places[k0 + r // (pairs * some), r // some % pairs, c0 + r % some] = n0 + r
     swapped = (lanes - EARLY) * pairs * chunks
-    ordered = [c for c in range(chunks) if c % own_chunks >= soon]
-    ordered = ordered + [c for c in range(chunks) if c not in ordered]
+    ordered = list(range(chunks))
     partner = [(c + own_chunks) % chunks for c in ordered]
     last = [[(k, c) for k in range(EARLY) for c in range(chunks) if (c % own_chunks < soon) == kind]
             for kind in (True, False)]
@@ -59,8 +58,8 @@
     piece = hpp * head
     per_kv = hp // kvh
     per_run = per_kv // hpp
-    each = -(-pieces // 3)
-    wait_for = own_chunks * pairs - 1
+    each = -(-pieces // 4)
+    wait_for = own_chunks * pairs - 2 if own_chunks > 1 else 1
     part = tokens // lanes
     a, g, s = lax.axis_index("grp"), lax.axis_index("kv"), lax.axis_index("srv")
     u, v = s // pairs, s % pairs

time: 113 us -> 113 us (level)
  no operation moved by 1% of the time
where the time goes in v6:
time: 113 us; the launch traced here: 112 us
  Pallas kernels  111 us (98%)
    pallas_call x1, Pallas kernels, on_device(): pl.pallas_call(functools.partial(layer, (head, heads, kvh, hp, hpp, halve...  111 us

profile of v6, /device:TPU:3, one launch (start us, length us, event | category | flops | bytes accessed | tf_op | source)
XLA Modules:
  0.0 111.6 jit_solution(2596966783270999111)
XLA Ops:
  0.0 110.6 %shard_map.55 = bf16[256,2048]{1,0:T(8,128)(2,1)S(1)} custom-call(s32[4]{0:T(128)} %lengths_in.1, bf16[256,4,512]{2,1,0:T(4,128)(2,1)} %q_hbm.1, bf16[256,4,128]{2,1,0:T(4,128)(2,1)} %k_hbm.1, bf16[256,4,128]{2,1,0:T(4,128)(2,1)} %v_hbm.1, bf16[2048,1024]{1,0:T(8,128)(2,1)} %bitcast.1), custom_call_target="tpu_custom_call" | custom-call | tf_op jit(solution)/shard_map/pallas_call | solution.py:581
  110.6 1.0 copy.7

commit v7 on v6

--- a/solution.py
+++ b/solution.py
@@ -144,11 +144,11 @@
     def query(j):
         size = per_kv * head
         return remote(q_ref.at[:, lane_at(ov * inner + j * size, size)],
-                      qbuf.at[0, :, pl.ds(j * size, size)], q_s.at[j], q_r.at[j], beside)
+                      qbuf.at[0, :, pl.ds(j * size, size)], q_s.at[0], q_r.at[j], beside)
 
     def weight(c):
         return remote(w_ref.at[pl.ds(ov * inner, inner), pl.ds(c * cw, cw)],
-                      wbuf.at[own_chunks + c], w_s.at[c], w_r.at[c], beside)
+                      wbuf.at[own_chunks + c], w_s.at[0], w_r.at[c], beside)
 
     def own_weight(c):
         return pltpu.make_async_copy(
@@ -530,14 +530,13 @@
 
     for j in range(kvh):
         kv_beside(j).wait_send()
-        query(j).wait_send()
         swap(0, 1, j, a).wait_send()
         for d in range(1, back + 1):
             for w in range(pairs):
                 pl.when((u >= d - 1) & right)(lambda d=d, w=w, j=j: kv_up(d, w, j).wait_send())
                 pl.when(u >= d)(lambda d=d, w=w, j=j: swap(d, w, j, a).wait_send())
-    for c in range(own_chunks):
-        weight(c).wait_send()
+    sent(qbuf.at[0], q_s.at[0])
+    sent(wbuf.at[pl.ds(0, own_chunks)], w_s.at[0])
     for d in range(1, lanes):
         for way in range(2):
             p = u - (d - 1) if way == 0 else u + (d - 1)
@@ -605,8 +604,8 @@
             pltpu.VMEM(((lanes - EARLY) * chunks, tokens // cores, cw), bf16),
             pltpu.VMEM((lanes * chunks, part, cw), bf16),
             dma((kvh,)), dma((kvh,)), dma((back, pairs, kvh)), dma((back, pairs, kvh)),
-            dma((2 * back + 1, kvh)), dma((2 * back + 1, kvh)), dma((kvh,)), dma((kvh,)),
-            dma((own_chunks,)), dma((own_chunks,)), dma((own_chunks,)),
+            dma((2 * back + 1, kvh)), dma((2 * back + 1, kvh)), dma((1,)), dma((kvh,)),
+            dma((own_chunks,)), dma((1,)), dma((own_chunks,)),
             dma((2, lanes - 1)), dma((2, lanes - 1, pieces)),
             dma((1,)), dma((RING,)), dma((1,)), dma((2 * RING,)),
             dma((2,)), dma((lanes * chunks,)), dma((1,)), dma((1,)),

time: 113 us -> 113 us (level)
  no operation moved by 1% of the time
where the time goes in v7:
time: 113 us; the launch traced here: 112 us
  Pallas kernels  111 us (98%)
    pallas_call x1, Pallas kernels, on_device(): pl.pallas_call(functools.partial(layer, (head, heads, kvh, hp, hpp, halve...  111 us

profile of v7, /device:TPU:3, one launch (start us, length us, event | category | flops | bytes accessed | tf_op | source)
XLA Modules:
  0.0 111.6 jit_solution(16902865555874971445)
XLA Ops:
  0.0 110.6 %shard_map.55 = bf16[256,2048]{1,0:T(8,128)(2,1)S(1)} custom-call(s32[4]{0:T(128)} %lengths_in.1, bf16[256,4,512]{2,1,0:T(4,128)(2,1)} %q_hbm.1, bf16[256,4,128]{2,1,0:T(4,128)(2,1)} %k_hbm.1, bf16[256,4,128]{2,1,0:T(4,128)(2,1)} %v_hbm.1, bf16[2048,1024]{1,0:T(8,128)(2,1)} %bitcast.1), custom_call_target="tpu_custom_call" | custom-call | tf_op jit(solution)/shard_map/pallas_call | solution.py:580
  110.6 1.0 copy.7
